TPU v7x, 512 devices: a whole 4x4x16 slice. The times are simulated.
512 devices in a mesh: theta: 64 (over z, y_hi, core), gz: 8 (over x, y_lo).
Axes of the slice: x: 4, y: 4 (y_hi: 2, y_lo: 2; y = y_hi * 2 + y_lo), z: 16, core: 2. Of those that a mesh axis runs over, the one named last changes fastest.
Arguments:
- fluid_state: float32 [8, 64, 1024, 128], P(None, 'gz', 'theta'), may hold values from -5 to 20, as said below
- levels: int32 [4, 128], P(None, 'theta'), may hold values from 0 to 1, as said below
- fine_rim: float32 [512, 2, 8, 1024], P('theta', None, None, 'gz'), may hold values from -1.5 to 3, as said below
- slot_owner: int32 [512], replicated, may hold values from 0 to 63, as said below
- slot_block: int32 [512], replicated, may hold values from 0 to 1
- slot_count: int32 [64], replicated, may hold values from 0 to 8, as said below
Outputs:
- residual: float32 [8, 64, 1024, 128], P(None, 'gz', 'theta')
- flux_mismatch: float32 [8, 64, 1024], P(None, 'gz', 'theta')
- inner_flux: float32 [8, 64, 1024], P(None, 'gz', 'theta')
Inputs may be any that keep to these rules, and one draw needn't show every extreme that they name: `fluid_state`: density and pressure are positive; velocities and fields up to 1.5 in magnitude. `fine_rim`: primitive variables: density and pressure positive, velocity and field components up to 1.5 in magnitude. `levels`: each column is 1 on its first r blocks and 0 after, with at least one 1 and one 0. `slot_owner`: slot d * 8 + s belongs to theta device d; the valid slots of a device are its first slot_count[d]; values of other slots are arbitrary; every pair of owner and block is named by exactly two valid slots. `slot_count`: some device fills all 8 slots in every draw.
All inputs are finite; a program needn't handle non-finite values.
Results may differ from a plain program's by a relative error of at most 0.0003.
Values sent between devices are 32-bit elements; how exact they have to be, the bound alone decides.
A program may use at most 64 MiB of HBM per device.

v0:
```python
import math
import jax
import jax.numpy as jnp
from jax import lax
from jax.sharding import PartitionSpec as P

BT = 8
BR = 32
GAMMA = 5.0 / 3.0
AXIS_FLIP = (1.0, -1.0, -1.0, 1.0, 1.0, -1.0, -1.0, 1.0)


def extended_2(cells, sides, width, closed):
    for axis, dim in sides:
        count = lax.axis_size(axis)
        ends = count if closed else count - 1
        head = lax.slice_in_dim(cells, 0, width, axis=dim)
        tail = lax.slice_in_dim(cells, cells.shape[dim] - width, cells.shape[dim], axis=dim)
        cells = jnp.concatenate(
            [
                lax.ppermute(tail, axis, [(i, (i + 1) % count) for i in range(ends)]),
                cells,
                lax.ppermute(head, axis, [((i + 1) % count, i) for i in range(ends)]),
            ],
            axis=dim,
        )
    return cells


def from_partner(block, axis, distance):
    count = lax.axis_size(axis)
    route = []
    for low in range(count):
        high = low | 1 << distance
        if high != low and high < count:
            route += [(low, high), (high, low)]
    return lax.ppermute(block, axis, route)


def primitive(conserved):
    density = conserved[0]
    vel_r = conserved[1] / density
    vel_t = conserved[2] / density
    vel_z = conserved[3] / density
    kinetic = 0.5 * density * (vel_r * vel_r + vel_t * vel_t + vel_z * vel_z)
    magnetic = 0.5 * (
        conserved[5] * conserved[5] + conserved[6] * conserved[6] + conserved[7] * conserved[7]
    )
    pressure = (GAMMA - 1.0) * (conserved[4] - kinetic - magnetic)
    return jnp.stack(
        [density, vel_r, vel_t, vel_z, pressure, conserved[5], conserved[6], conserved[7]]
    )


def physical(states, normal):
    density = states[0]
    velocity = (states[1], states[2], states[3])
    pressure = states[4]
    field = (states[5], states[6], states[7])
    vel_n = velocity[normal]
    field_n = field[normal]
    field_sq = field[0] * field[0] + field[1] * field[1] + field[2] * field[2]
    speed_sq = velocity[0] * velocity[0] + velocity[1] * velocity[1] + velocity[2] * velocity[2]
    vel_dot = velocity[0] * field[0] + velocity[1] * field[1] + velocity[2] * field[2]
    total_p = pressure + 0.5 * field_sq
    energy = pressure / (GAMMA - 1.0) + 0.5 * density * speed_sq + 0.5 * field_sq
    conserved = jnp.stack(
        [
            density,
            density * velocity[0],
            density * velocity[1],
            density * velocity[2],
            energy,
            field[0],
            field[1],
            field[2],
        ]
    )
    momentum = [
        density * velocity[component] * vel_n
        - field[component] * field_n
        + (total_p if component == normal else 0.0)
        for component in (0, 1, 2)
    ]
    induction = [
        vel_n * field[component] - field_n * velocity[component] for component in (0, 1, 2)
    ]
    fluxes = jnp.stack(
        [density * vel_n] + momentum + [(energy + total_p) * vel_n - field_n * vel_dot] + induction
    )
    signal = jnp.abs(vel_n) + jnp.sqrt((GAMMA * pressure + field_sq) / density)
    return (conserved, fluxes, signal)


def rusanov(left_state, right_state, normal):
    cons_left, flux_left, signal_left = physical(left_state, normal)
    cons_right, flux_right, signal_right = physical(right_state, normal)
    return 0.5 * (flux_left + flux_right) - 0.5 * jnp.maximum(signal_left, signal_right) * (
        cons_right - cons_left
    )


def minmod(lower_diff, upper_diff):
    return (
        0.5
        * (jnp.sign(lower_diff) + jnp.sign(upper_diff))
        * jnp.minimum(jnp.abs(lower_diff), jnp.abs(upper_diff))
    )


def face_pairs(extended, axis_dim, length):
    middle = lax.slice_in_dim(extended, 1, length + 3, axis=axis_dim)
    behind = lax.slice_in_dim(extended, 0, length + 2, axis=axis_dim)
    beyond = lax.slice_in_dim(extended, 2, length + 4, axis=axis_dim)
    slopes = minmod(middle - behind, beyond - middle)
    left_state = lax.slice_in_dim(middle + 0.5 * slopes, 0, length + 1, axis=axis_dim)
    right_state = lax.slice_in_dim(middle - 0.5 * slopes, 1, length + 2, axis=axis_dim)
    return (left_state, right_state)


def local_residual(conserved, theta_ext, axial_ext, partner_row, dtheta):
    fields, depth_z, width_t, radial = conserved.shape
    states = primitive(conserved)
    theta_states = jnp.concatenate(
        [primitive(theta_ext[:, :, :2]), states, primitive(theta_ext[:, :, -2:])], axis=2
    )
    axial_states = jnp.concatenate(
        [primitive(axial_ext[:, :2]), states, primitive(axial_ext[:, -2:])], axis=1
    )
    flipper = jnp.array(AXIS_FLIP, jnp.float32).reshape(-1, 1, 1)
    across = primitive(partner_row) * flipper
    behind = jnp.concatenate([across[..., None], states[..., :-1]], axis=-1)
    beyond = jnp.concatenate([states[..., 1:], states[..., -1:]], axis=-1)
    slopes = minmod(states - behind, beyond - states)
    left_state = states + 0.5 * slopes
    right_state = jnp.concatenate([(states - 0.5 * slopes)[..., 1:], states[..., -1:]], axis=-1)
    radial_flux = rusanov(left_state, right_state, 0)
    face_radius = jnp.arange(radial, dtype=jnp.float32) + 1.0
    cell_radius = jnp.arange(radial, dtype=jnp.float32) + 0.5
    outward = radial_flux * (face_radius * dtheta)
    inward = jnp.concatenate([jnp.zeros_like(outward[..., :1]), outward[..., :-1]], axis=-1)
    theta_left, theta_right = face_pairs(theta_states, 2, width_t)
    theta_flux = rusanov(theta_left, theta_right, 1)
    axial_left, axial_right = face_pairs(axial_states, 1, depth_z)
    axial_flux = rusanov(axial_left, axial_right, 2)
    residual = (
        inward
        - outward
        - (theta_flux[:, :, 1:] - theta_flux[:, :, :-1])
        - (axial_flux[:, 1:] - axial_flux[:, :-1]) * (cell_radius * dtheta)
    )
    density = states[0]
    vel_r = states[1]
    vel_t = states[2]
    pressure = states[4]
    field_r = states[5]
    field_t = states[6]
    field_sq = states[5] * states[5] + states[6] * states[6] + states[7] * states[7]
    residual = residual.at[1].add(
        dtheta * (density * vel_t * vel_t + pressure + 0.5 * field_sq - field_t * field_t)
    )
    residual = residual.at[2].add(-dtheta * (density * vel_r * vel_t - field_r * field_t))
    residual = residual.at[6].add(dtheta * (vel_r * field_t - vel_t * field_r))
    return (residual, radial_flux)


def reflux(residual, radial_flux, fine_cells, face_index, dtheta):
    radial = residual.shape[-1]
    positions = jnp.arange(radial, dtype=jnp.int32)
    pick_face = (positions[None, :] == (face_index - 1)[:, None]).astype(jnp.float32)
    coarse_face = jnp.sum(radial_flux * pick_face, axis=-1)
    mismatch = fine_cells - coarse_face
    area = face_index.astype(jnp.float32) * dtheta
    correction = area * mismatch
    outer_cell = (positions[None, :] == face_index[:, None]).astype(jnp.float32)
    volume = (jnp.arange(radial, dtype=jnp.float32) + 0.5) * dtheta
    return ((residual + correction[..., None] * outer_cell) / volume, mismatch)


def fine_faces(fine_rim):
    rim_states = jnp.moveaxis(fine_rim, 2, 0)
    flux_out = rusanov(rim_states[:, :, 0], rim_states[:, :, 1], 0)
    fields, slot_total, length = flux_out.shape
    paired = flux_out.reshape(fields, slot_total, length // (2 * BT), BT, 2)
    return 0.25 * jnp.sum(paired, axis=-1)


def body(fluid_state, levels, fine_rim, slot_owner, slot_block, slot_count):
    fields, depth_z, width_t, radial = fluid_state.shape
    devices = lax.axis_size("theta")
    dtheta = 2.0 * math.pi / (width_t * devices)
    theta_pos = lax.axis_index("theta")
    theta_ext = extended_2(fluid_state, (("theta", 2),), 2, True)
    axial_raw = extended_2(fluid_state, (("gz", 1),), 2, False)
    axial_pos = lax.axis_index("gz")
    ghost_shape = (fields, 2, width_t, radial)
    bottom = jnp.where(
        axial_pos == 0, jnp.broadcast_to(fluid_state[:, :1], ghost_shape), axial_raw[:, :2]
    )
    upper_ghost = jnp.where(
        axial_pos == lax.axis_size("gz") - 1,
        jnp.broadcast_to(fluid_state[:, -1:], ghost_shape),
        axial_raw[:, -2:],
    )
    axial_ext = jnp.concatenate([bottom, fluid_state, upper_ghost], axis=1)
    first_row = fluid_state[..., 0].reshape(fields, depth_z * width_t)
    across = from_partner(first_row, "theta", devices.bit_length() - 2)
    partner_row = across.reshape(fields, depth_z, width_t)
    residual, radial_flux = local_residual(fluid_state, theta_ext, axial_ext, partner_row, dtheta)
    partials = fine_faces(fine_rim)
    slot_cap = fine_rim.shape[0]
    live_slots = (jnp.arange(slot_cap, dtype=jnp.int32) < slot_count[theta_pos]).astype(jnp.float32)
    partials = partials * live_slots[None, :, None, None]
    rows_out = jnp.moveaxis(partials, 1, 0).reshape(slot_cap, fields * depth_z * BT)
    blocks_dev = width_t // BT
    chosen = (
        (slot_owner == theta_pos)[None, :]
        & (slot_block[None, :] == jnp.arange(blocks_dev, dtype=jnp.int32)[:, None])
    ).astype(jnp.float32)
    registers = jnp.dot(
        chosen,
        lax.all_gather(rows_out, "theta", axis=0, tiled=True),
        precision=lax.Precision.HIGHEST,
    )
    fine_cells = (
        registers.reshape(blocks_dev, fields, depth_z, BT)
        .transpose(1, 2, 0, 3)
        .reshape(fields, depth_z, width_t)
    )
    face_index = jnp.repeat(BR * jnp.sum(levels, axis=0), BT)
    result, mismatch = reflux(residual, radial_flux, fine_cells, face_index, dtheta)
    return (result, mismatch, radial_flux[..., 0])


def solution(mesh):
    return jax.shard_map(
        body,
        mesh=mesh,
        in_specs=(
            P(None, "gz", "theta", None),
            P(None, "theta"),
            P("theta", None, None, "gz"),
            P(),
            P(),
            P(),
        ),
        out_specs=(P(None, "gz", "theta", None), P(None, "gz", "theta"), P(None, "gz", "theta")),
        check_vma=False,
    )
```

profile of v0, /device:TPU:1, one launch (start us, length us, event | category | flops | bytes accessed | tf_op | source)
XLA Modules:
  0.0 194.4 jit_solution(17062907998773435416)
XLA Ops:
  7.2 1.7 fusion.64
  9.0 1.3 collective-permute-start.4
  10.2 5.3 %collective-permute-start.3 = (f32[8,2,16,128]{3,2,1,0:T(8,128)}, f32[8,2,16,128]{3,2,1,0:T(8,128)}, u32[]{:S(2)}, u32[]{:S(2)}) collective-permute-start(f32[8,2,16,128]{3,2,1,0:T(8,128)} %get-tuple-element.146), channel_id=1, source_target_pairs={{0,1},{1,2},{2,3},{3,4},{4,5},{5,6},{6,7},{8,9},{9,10},{10,11},{11... | collective-permute-start | bytes 393224 | tf_op jit(solution)/shard_map/ppermute | solution.py:21
  15.6 0.6 copy.490
  16.2 8.7 %collective-permute-start.2 = (f32[8,8,2,128]{3,1,2,0:T(8,128)}, f32[8,8,2,128]{3,1,2,0:T(8,128)S(1)}, u32[]{:S(2)}, u32[]{:S(2)}) collective-permute-start(f32[8,8,2,128]{3,1,2,0:T(8,128)} %copy.490), channel_id=1, source_target_pairs={{8,0},{16,8},{24,16},{32,24},{40,32},{48,40},{56,48},{64,56},{72,6... | collective-permute-start | bytes 196616 | tf_op jit(solution)/shard_map/ppermute | solution.py:23
  24.9 0.6 copy.489
  25.6 1.9 collective-permute-start.1
  27.8 12.9 %collective-permute-start = (f32[8,128]{1,0:T(8,128)S(1)}, f32[8,128]{1,0:T(8,128)S(1)}, u32[]{:S(2)}, u32[]{:S(2)}) collective-permute-start(f32[8,128]{1,0:T(8,128)S(1)} %reshape_squeeze.3), channel_id=1, source_target_pairs={{0,256},{256,0},{8,264},{264,8},{16,272},{272,16},{24,280},{280,24... | collective-permute-start | bytes 12296 | tf_op jit(solution)/shard_map/ppermute | solution.py:37
  45.1 0.6 copy-done.11
  46.4 0.6 compare_select_fusion
  47.0 0.7 copy.487
  49.5 0.7 constant_dynamic-update-slice_fusion.1
  50.2 1.0 fusion.62
  53.2 0.7 slice_reduce_fusion.2
  54.6 0.6 copy-done.10
  55.2 0.7 broadcast_multiply_fusion.2
  55.9 1.2 copy.359
  57.1 1.6 fusion.61
  60.4 0.7 copy-done.4
  61.1 0.8 slice_reduce_fusion
  63.6 0.9 broadcast_select_fusion
  67.7 115.7 %all-gather.2.cloned.1.call-done = f32[512,512]{1,0:T(8,128)} async-done(((f32[8,512]{1,0:T(8,128)}), f32[512,512]{1,0:T(8,128)}) %all-gather.2.cloned.1.call-update) | async-done | bytes 1048592 | tf_op jit(solution)/shard_map/all_gather | solution.py:222
  183.4 1.7 fusion.47
  186.6 1.0 add_divide_fusion
  (231 shorter events, 16.8 us)
Async XLA Ops:
  7.2 8.4 %copy-start = (f32[8,8,16,128]{3,2,1,0:T(8,128)S(1)}, f32[8,8,16,128]{3,2,1,0:T(8,128)}, u32[]{:S(2)}) copy-start(f32[8,8,16,128]{3,2,1,0:T(8,128)} %param.13) | copy-start | bytes 1572868
  7.2 176.2 %all-gather.2.cloned.1.call-start = ((), (), s32[]{:S(2)}) async-start(), calls=%async_computation | async-start | bytes 1064960 | tf_op jit(solution)/shard_map/all_gather | solution.py:222
  9.0 54.6 %collective-permute-start.4 = (f32[8,2,16,128]{3,2,1,0:T(8,128)}, f32[8,2,16,128]{3,2,1,0:T(8,128)}, u32[]{:S(2)}, u32[]{:S(2)}) collective-permute-start(f32[8,2,16,128]{3,2,1,0:T(8,128)} %get-tuple-element.147), channel_id=1, source_target_pairs={{1,0},{2,1},{3,2},{4,3},{5,4},{6,5},{7,6},{9,8},{10,9},{11,10},{12... | collective-permute-start | bytes 393224 | tf_op jit(solution)/shard_map/ppermute | solution.py:23
  10.2 54.3 %collective-permute-start.3 = (f32[8,2,16,128]{3,2,1,0:T(8,128)}, f32[8,2,16,128]{3,2,1,0:T(8,128)}, u32[]{:S(2)}, u32[]{:S(2)}) collective-permute-start(f32[8,2,16,128]{3,2,1,0:T(8,128)} %get-tuple-element.146), channel_id=1, source_target_pairs={{0,1},{1,2},{2,3},{3,4},{4,5},{5,6},{6,7},{8,9},{9,10},{10,11},{11... | collective-permute-start | bytes 393224 | tf_op jit(solution)/shard_map/ppermute | solution.py:21
  16.2 45.7 %collective-permute-start.2 = (f32[8,8,2,128]{3,1,2,0:T(8,128)}, f32[8,8,2,128]{3,1,2,0:T(8,128)S(1)}, u32[]{:S(2)}, u32[]{:S(2)}) collective-permute-start(f32[8,8,2,128]{3,1,2,0:T(8,128)} %copy.490), channel_id=1, source_target_pairs={{8,0},{16,8},{24,16},{32,24},{40,32},{48,40},{56,48},{64,56},{72,6... | collective-permute-start | bytes 196616 | tf_op jit(solution)/shard_map/ppermute | solution.py:23
  25.6 36.4 %collective-permute-start.1 = (f32[8,8,2,128]{3,1,2,0:T(8,128)}, f32[8,8,2,128]{3,1,2,0:T(8,128)S(1)}, u32[]{:S(2)}, u32[]{:S(2)}) collective-permute-start(f32[8,8,2,128]{3,1,2,0:T(8,128)} %copy.489), channel_id=1, source_target_pairs={{0,8},{8,16},{16,24},{24,32},{32,40},{40,48},{48,56},{56,64},{64,7... | collective-permute-start | bytes 196616 | tf_op jit(solution)/shard_map/ppermute | solution.py:21
  27.5 13.2 %copy-start.2 = (f32[8,2,8,128]{3,2,1,0:T(8,128)S(1)}, f32[8,2,8,128]{3,2,1,0:T(8,128)}, u32[]{:S(2)}) copy-start(f32[8,2,8,128]{3,2,1,0:T(8,128)} %param.15) | copy-start | bytes 196612
  27.8 24.9 %collective-permute-start = (f32[8,128]{1,0:T(8,128)S(1)}, f32[8,128]{1,0:T(8,128)S(1)}, u32[]{:S(2)}, u32[]{:S(2)}) collective-permute-start(f32[8,128]{1,0:T(8,128)S(1)} %reshape_squeeze.3), channel_id=1, source_target_pairs={{0,256},{256,0},{8,264},{264,8},{16,272},{272,16},{24,280},{280,24... | collective-permute-start | bytes 12296 | tf_op jit(solution)/shard_map/ppermute | solution.py:37
  45.1 0.7 copy-start.11
  47.8 0.7 copy-start.8
  50.2 1.0 copy-start.7
  54.6 0.7 copy-start.10
  60.4 0.7 copy-start.4
  66.1 0.6 copy-start.5
  66.7 0.8 copy-start.1
  67.6 115.8 %copy-start.3 = (s32[512]{0:T(512)S(1)}, s32[512]{0:T(512)}, u32[]{:S(2)}) copy-start(s32[512]{0:T(512)} %param.17) | copy-start | bytes 6148
  67.6 115.8 %copy-start.6 = (pred[512]{0:T(512)(128)(4,1)S(1)}, pred[512]{0:T(512)(128)(4,1)}, u32[]{:S(2)}) copy-start(pred[512]{0:T(512)(128)(4,1)} %broadcast_compare_fusion) | copy-start | bytes 1540
  185.3 0.6 copy-start.9
Sparse Core Ops, SparseCore 0:
  47.9 135.4 all-gather.1
where the time goes:
time: 195 us; the launch traced here: 194 us
  waiting for transfers between devices  116 us (59%)
  starting transfers between devices  30.1 us (15%)
  local copies, waits for them, and re-layouts  17.2 us (9%)
  between operations  15.3 us (8%)
  other arithmetic  14.4 us (7%)
    all_gather x1, waiting for transfers between devices, body(): lax.all_gather(rows_out, 'theta', axis=0, tiled=True)  116 us
    ppermute x1, starting transfers between devices, from_partner(): return lax.ppermute(block, axis, route)  12.9 us
    ppermute x2, starting transfers between devices, extended_2(): lax.ppermute(head, axis, [((i + 1) % count, i) for i in range(ends)])  9.94 us
    ppermute x2, starting transfers between devices, extended_2(): lax.ppermute(tail, axis, [(i, (i + 1) % count) for i in range(ends)])  7.23 us
    unnamed x45, local copies, waits for them, and re-layouts  5.39 us
  transfers between devices with their start and end apart: 6, of which 1 were waited for; matrix products, arithmetic and copies ran while one was open for 12% of the time, Pallas kernels for 0%

commit v1 on v0

--- a/solution.py
+++ b/solution.py
@@ -186,6 +186,12 @@
 
 
 def body(fluid_state, levels, fine_rim, slot_owner, slot_block, slot_count):
+
+    def mark_the_stocks(here_x):
+        seen_now = jnp.stack([here_x for _ in range(lax.psum(1, "theta"))], 0)
+        state_now = lax.all_to_all(seen_now, "theta", 0, 0)
+        return jnp.concatenate(state_now, 0)
+
     fields, depth_z, width_t, radial = fluid_state.shape
     devices = lax.axis_size("theta")
     dtheta = 2.0 * math.pi / (width_t * devices)
@@ -217,11 +223,7 @@
         (slot_owner == theta_pos)[None, :]
         & (slot_block[None, :] == jnp.arange(blocks_dev, dtype=jnp.int32)[:, None])
     ).astype(jnp.float32)
-    registers = jnp.dot(
-        chosen,
-        lax.all_gather(rows_out, "theta", axis=0, tiled=True),
-        precision=lax.Precision.HIGHEST,
-    )
+    registers = jnp.dot(chosen, mark_the_stocks(rows_out), precision=lax.Precision.HIGHEST)
     fine_cells = (
         registers.reshape(blocks_dev, fields, depth_z, BT)
         .transpose(1, 2, 0, 3)

time: 195 us -> 115 us (0.59)
  waiting for transfers between devices: 116 us -> 13 us
  local copies, waits for them, and re-layouts: 17.2 us -> 35.9 us
  between operations: 15.3 us -> 1.85 us
  starting transfers between devices: 30.1 us -> 39.7 us
  other arithmetic: 14.4 us -> 19 us
    all_gather x1 -> x0, waiting for transfers between devices: 116 us -> none  [body(): lax.all_gather(rows_out, 'theta', axis=0, tiled=True)]
    all_to_all x0 -> x1, waiting for transfers between devices: none -> 12.9 us  [mark_the_stocks(): state_now = lax.all_to_all(seen_now, 'theta', 0, 0)]
    another operation x15, local copies, waits for them, and re-layouts: 0.82 us -> 11.2 us  [primitive(): jnp.stack([density, vel_r, vel_t, vel_z, pressure, conserved[5], conserve...]
    all_to_all x0 -> x1, starting transfers between devices: none -> 9.64 us  [mark_the_stocks(): state_now = lax.all_to_all(seen_now, 'theta', 0, 0)]
    unnamed x45 -> x59, local copies, waits for them, and re-layouts: 5.39 us -> 11.4 us
  transfers between devices with their start and end apart: 6 -> 6, of which waited for: 1 -> 1; matrix products, arithmetic and copies ran while one was open for 12% -> 41% of each run, Pallas kernels for 0% -> 0%
where the time goes in v1:
time: 115 us; the launch traced here: 113 us
  starting transfers between devices  39.7 us (35%)
  local copies, waits for them, and re-layouts  35.9 us (31%)
  other arithmetic  19 us (17%)
  waiting for transfers between devices  13 us (11%)
  matrix products  3.55 us (3%)
  between operations  1.85 us (2%)
    all_to_all x1, waiting for transfers between devices, mark_the_stocks(): state_now = lax.all_to_all(seen_now, 'theta', 0, 0)  12.9 us
    ppermute x1, starting transfers between devices, from_partner(): return lax.ppermute(block, axis, route)  12.9 us
    unnamed x59, local copies, waits for them, and re-layouts  11.4 us
    another operation x15, local copies, waits for them, and re-layouts, primitive(): jnp.stack([density, vel_r, vel_t, vel_z, pressure, conserved[5], conserve...  11.2 us
    ppermute x2, starting transfers between devices, extended_2(): lax.ppermute(head, axis, [((i + 1) % count, i) for i in range(ends)])  9.94 us
    all_to_all x1, starting transfers between devices, mark_the_stocks(): state_now = lax.all_to_all(seen_now, 'theta', 0, 0)  9.64 us
    ppermute x2, starting transfers between devices, extended_2(): lax.ppermute(tail, axis, [(i, (i + 1) % count) for i in range(ends)])  7.24 us
    dot_general x1, matrix products, body(): jnp.dot(chosen, mark_the_stocks(rows_out), precision=lax.Precision.HIGHEST)  3.55 us
  transfers between devices with their start and end apart: 6, of which 1 were waited for; matrix products, arithmetic and copies ran while one was open for 41% of the time, Pallas kernels for 0%

profile of v1, /device:TPU:1, one launch (start us, length us, event | category | flops | bytes accessed | tf_op | source)
XLA Modules:
  0.0 113.0 jit_solution(13623816264367172926)
XLA Ops:
  0.6 1.8 %fusion.64 = (f32[8,2,16,128]{3,2,1,0:T(8,128)}, f32[8,2,16,128]{3,2,1,0:T(8,128)}) fusion(f32[8,8,16,128]{3,2,1,0:T(8,128)} %param.13), kind=kLoop, calls=%fused_computation.363 | loop fusion | bytes 524288 | tf_op jit(solution)/shard_map/slice | solution.py:18
  2.4 1.3 %collective-permute-start.4 = (f32[8,2,16,128]{3,2,1,0:T(8,128)}, f32[8,2,16,128]{3,2,1,0:T(8,128)}, u32[]{:S(2)}, u32[]{:S(2)}) collective-permute-start(f32[8,2,16,128]{3,2,1,0:T(8,128)} %get-tuple-element.147), channel_id=1, source_target_pairs={{1,0},{2,1},{3,2},{4,3},{5,4},{6,5},{7,6},{9,8},{10,9},{11,10},{12... | collective-permute-start | bytes 393224 | tf_op jit(solution)/shard_map/ppermute | solution.py:23
  3.7 5.3 %collective-permute-start.3 = (f32[8,2,16,128]{3,2,1,0:T(8,128)}, f32[8,2,16,128]{3,2,1,0:T(8,128)}, u32[]{:S(2)}, u32[]{:S(2)}) collective-permute-start(f32[8,2,16,128]{3,2,1,0:T(8,128)} %get-tuple-element.146), channel_id=1, source_target_pairs={{0,1},{1,2},{2,3},{3,4},{4,5},{5,6},{6,7},{8,9},{9,10},{10,11},{11... | collective-permute-start | bytes 393224 | tf_op jit(solution)/shard_map/ppermute | solution.py:21
  9.7 8.7 %collective-permute-start.2 = (f32[8,8,2,128]{3,1,2,0:T(8,128)}, f32[8,8,2,128]{3,1,2,0:T(8,128)S(1)}, u32[]{:S(2)}, u32[]{:S(2)}) collective-permute-start(f32[8,8,2,128]{3,1,2,0:T(8,128)} %copy.489), channel_id=1, source_target_pairs={{8,0},{16,8},{24,16},{32,24},{40,32},{48,40},{56,48},{64,56},{72,6... | collective-permute-start | bytes 196616 | tf_op jit(solution)/shard_map/ppermute | solution.py:23
  19.0 1.9 %collective-permute-start.1 = (f32[8,8,2,128]{3,1,2,0:T(8,128)}, f32[8,8,2,128]{3,1,2,0:T(8,128)S(1)}, u32[]{:S(2)}, u32[]{:S(2)}) collective-permute-start(f32[8,8,2,128]{3,1,2,0:T(8,128)} %copy.488), channel_id=1, source_target_pairs={{0,8},{8,16},{16,24},{24,32},{32,40},{40,48},{48,56},{56,64},{64,7... | collective-permute-start | bytes 196616 | tf_op jit(solution)/shard_map/ppermute | solution.py:21
  21.8 12.9 %collective-permute-start = (f32[8,128]{1,0:T(8,128)}, f32[8,128]{1,0:T(8,128)}, u32[]{:S(2)}, u32[]{:S(2)}) collective-permute-start(f32[8,128]{1,0:T(8,128)} %reshape_squeeze.3), channel_id=1, source_target_pairs={{0,256},{256,0},{8,264},{264,8},{16,272},{272,16},{24,280},{280,24... | collective-permute-start | bytes 12296 | tf_op jit(solution)/shard_map/ppermute | solution.py:37
  42.3 9.6 %all-to-all-start = ((f32[64,8,512]{2,1,0:T(8,128)}), f32[64,8,512]{2,1,0:T(8,128)S(1)}, u32[]{:S(2)}, u32[]{:S(2)}) async-start(f32[64,8,512]{2,1,0:T(8,128)} %stack.103), calls=%async_computation | async-start | bytes 2097152 | tf_op jit(solution)/shard_map/all_to_all | solution.py:192
  57.1 1.4 %slice_divide_fusion.17 = (f32[1,128]{1,0:T(1,128)}, f32[1,128]{1,0:T(1,128)}, f32[1,128]{1,0:T(1,128)}) fusion(f32[8,128]{1,0:T(8,128)} %collective-permute-done), kind=kLoop, calls=%fused_computation.353 | loop fusion | flops 384 | bytes 3584 | tf_op jit(solution)/shard_map/div | solution.py:42
  59.0 2.1 %slice_reduce_fusion.2 = (f32[128]{0:T(128)}, f32[128]{0:T(128)}, f32[128]{0:T(128)}, f32[128]{0:T(128)}, f32[128]{0:T(128)}, /*index=5*/f32[128]{0:T(128)}, f32[128]{0:T(128)}, f32[128]{0:T(128)}) fusion(f32[8,128]{1,0:T(8,128)} %collective-permute-done, f32[1,128]{1,0:T(1,128)} %get-tuple-element.198, f32[1,128]{1,0:T(1,128)} %get-tuple-element.199, ...), kind=kLoop, calls=%fused_computation.354 | loop fusion | flops 2048 | bytes 8196 | tf_op jit(solution)/shard_map/slice | solution.py:47
  61.1 1.3 %stack.74 = f32[1,8,16,1]{2,1,3,0:T(8,128)} reshape(f32[128]{0:T(128)} %get-tuple-element.58) | data formatting | bytes 1024 | tf_op jit(solution)/shard_map/stack | solution.py:50
  62.4 1.3 %constant_dynamic-update-slice_fusion.13 = f32[8,8,16,1]{2,1,3,0:T(8,128)} fusion(f32[1,8,16,1]{2,1,3,0:T(8,128)} %stack.74), kind=kLoop, calls=%fused_computation.50 | loop fusion | bytes 4608
  63.7 1.3 %stack.75 = f32[1,8,16,1]{2,1,3,0:T(8,128)} reshape(f32[128]{0:T(128)} %get-tuple-element.59) | data formatting | bytes 1024 | tf_op jit(solution)/shard_map/stack | solution.py:50
  65.0 1.3 %stack.76 = f32[1,8,16,1]{2,1,3,0:T(8,128)} reshape(f32[128]{0:T(128)} %get-tuple-element.60) | data formatting | bytes 1024 | tf_op jit(solution)/shard_map/stack | solution.py:50
  66.3 1.3 %stack.77 = f32[1,8,16,1]{2,1,3,0:T(8,128)} reshape(f32[128]{0:T(128)} %get-tuple-element.61) | data formatting | bytes 1024 | tf_op jit(solution)/shard_map/stack | solution.py:50
  67.6 1.3 %stack.78 = f32[1,8,16,1]{2,1,3,0:T(8,128)} reshape(f32[128]{0:T(128)} %get-tuple-element.57) | data formatting | bytes 1024 | tf_op jit(solution)/shard_map/stack | solution.py:50
  69.0 1.2 %stack.79 = f32[1,8,16,1]{2,1,3,0:T(8,128)} reshape(f32[128]{0:T(128)} %get-tuple-element.56) | data formatting | bytes 1024 | tf_op jit(solution)/shard_map/stack | solution.py:50
  70.2 1.3 %stack.80 = f32[1,8,16,1]{2,1,3,0:T(8,128)} reshape(f32[128]{0:T(128)} %get-tuple-element.55) | data formatting | bytes 1024 | tf_op jit(solution)/shard_map/stack | solution.py:50
  71.5 1.3 %stack.81 = f32[1,8,16,1]{2,1,3,0:T(8,128)} reshape(f32[128]{0:T(128)} %get-tuple-element.54) | data formatting | bytes 1024 | tf_op jit(solution)/shard_map/stack | solution.py:50
  72.8 1.3 %constant_dynamic-update-slice_fusion.12 = f32[8,8,16,1]{2,1,3,0:T(8,128)} fusion(f32[8,8,16,1]{2,1,3,0:T(8,128)} %constant_dynamic-update-slice_fusion.13, f32[1,8,16,1]{2,1,3,0:T(8,128)} %stack.75), kind=kLoop, calls=%fused_computation.49 | loop fusion | bytes 8192
  78.1 1.4 %broadcast_multiply_fusion.2 = f32[8,8,16,1]{2,1,3,0:T(8,128)} fusion(f32[8,8,16,1]{2,1,3,0:T(8,128)} %constant_dynamic-update-slice_fusion.6, f32[8]{0:T(128)S(1)} %copy-done.17), kind=kLoop, calls=%fused_computation.308 | loop fusion | flops 1024 | bytes 8224 | tf_op jit(solution)/shard_map/mul | solution.py:131
  79.6 2.0 %copy.358 = f32[8,8,16,1]{3,2,1,0:T(8,128)} copy(f32[8,8,16,1]{2,1,3,0:T(8,128)} %broadcast_multiply_fusion.2) | data formatting | bytes 8192 | tf_op jit(solution)/shard_map/mul | solution.py:131
  81.6 1.9 %fusion.61 = (f32[8,8,16,128]{3,2,1,0:T(8,128)S(1)}, f32[8,8,16,128]{3,2,1,0:T(8,128)S(1)}) fusion(f32[8,8,16,128]{3,2,1,0:T(8,128)S(1)} %constant_dynamic-update-slice_fusion, f32[8,8,16,1]{3,2,1,0:T(8,128)S(1)} %slice.777, f32[8,8,16,127]{3,2,1,0:T(8,128)} %get-tuple-element.141, f32[8,8,16,127]{3,2,1,0:T(8,128)} %get-tuple-element.140, ...), kind=kLoop, calls=%fused_computation.360 | loop fusion | flops 1835008 | bytes 2621440 | tf_op jit(solution)/shard_map/add | solution.py:135
  93.0 12.9 %all-to-all-done = f32[64,8,512]{2,1,0:T(8,128)S(1)} async-done(((f32[64,8,512]{2,1,0:T(8,128)}), f32[64,8,512]{2,1,0:T(8,128)S(1)}, u32[]{:S(2)}, u32[]{:S(2)}) %all-to-all-start) | async-done | bytes 1048608 | tf_op jit(solution)/shard_map/all_to_all | solution.py:192
  107.0 3.5 %convolution_bitcast_fusion = f32[8,8,2,8]{3,2,1,0:T(2,128)S(1)} fusion(f32[8,8,8,512]{3,2,1,0:T(8,128)S(1)} %bitcast.48, pred[512]{0:T(512)(128)(4,1)S(1)} %copy-done.13, s32[512]{0:T(512)S(1)} %copy-done.10), kind=kOutput, calls=%fused_computation | convolution fusion | flops 6293504 | bytes 1055232 | tf_op jit(solution)/shard_map/dot_general | solution.py:226
  (244 shorter events, 31.3 us)
Async XLA Ops:
  0.6 8.4 %copy-start = (f32[8,8,16,128]{3,2,1,0:T(8,128)S(1)}, f32[8,8,16,128]{3,2,1,0:T(8,128)}, u32[]{:S(2)}) copy-start(f32[8,8,16,128]{3,2,1,0:T(8,128)} %param.13) | copy-start | bytes 1572868
  2.4 86.5 %collective-permute-start.4 = (f32[8,2,16,128]{3,2,1,0:T(8,128)}, f32[8,2,16,128]{3,2,1,0:T(8,128)}, u32[]{:S(2)}, u32[]{:S(2)}) collective-permute-start(f32[8,2,16,128]{3,2,1,0:T(8,128)} %get-tuple-element.147), channel_id=1, source_target_pairs={{1,0},{2,1},{3,2},{4,3},{5,4},{6,5},{7,6},{9,8},{10,9},{11,10},{12... | collective-permute-start | bytes 393224 | tf_op jit(solution)/shard_map/ppermute | solution.py:23
  3.7 86.3 %collective-permute-start.3 = (f32[8,2,16,128]{3,2,1,0:T(8,128)}, f32[8,2,16,128]{3,2,1,0:T(8,128)}, u32[]{:S(2)}, u32[]{:S(2)}) collective-permute-start(f32[8,2,16,128]{3,2,1,0:T(8,128)} %get-tuple-element.146), channel_id=1, source_target_pairs={{0,1},{1,2},{2,3},{3,4},{4,5},{5,6},{6,7},{8,9},{9,10},{10,11},{11... | collective-permute-start | bytes 393224 | tf_op jit(solution)/shard_map/ppermute | solution.py:21
  9.7 77.5 %collective-permute-start.2 = (f32[8,8,2,128]{3,1,2,0:T(8,128)}, f32[8,8,2,128]{3,1,2,0:T(8,128)S(1)}, u32[]{:S(2)}, u32[]{:S(2)}) collective-permute-start(f32[8,8,2,128]{3,1,2,0:T(8,128)} %copy.489), channel_id=1, source_target_pairs={{8,0},{16,8},{24,16},{32,24},{40,32},{48,40},{56,48},{64,56},{72,6... | collective-permute-start | bytes 196616 | tf_op jit(solution)/shard_map/ppermute | solution.py:23
  19.0 68.3 %collective-permute-start.1 = (f32[8,8,2,128]{3,1,2,0:T(8,128)}, f32[8,8,2,128]{3,1,2,0:T(8,128)S(1)}, u32[]{:S(2)}, u32[]{:S(2)}) collective-permute-start(f32[8,8,2,128]{3,1,2,0:T(8,128)} %copy.488), channel_id=1, source_target_pairs={{0,8},{8,16},{16,24},{24,32},{32,40},{40,48},{48,56},{56,64},{64,7... | collective-permute-start | bytes 196616 | tf_op jit(solution)/shard_map/ppermute | solution.py:21
  20.9 13.8 %copy-start.3 = (f32[8,2,8,128]{3,2,1,0:T(8,128)S(1)}, f32[8,2,8,128]{3,2,1,0:T(8,128)}, u32[]{:S(2)}) copy-start(f32[8,2,8,128]{3,2,1,0:T(8,128)} %param.15) | copy-start | bytes 196612
  21.8 35.3 %collective-permute-start = (f32[8,128]{1,0:T(8,128)}, f32[8,128]{1,0:T(8,128)}, u32[]{:S(2)}, u32[]{:S(2)}) collective-permute-start(f32[8,128]{1,0:T(8,128)} %reshape_squeeze.3), channel_id=1, source_target_pairs={{0,256},{256,0},{8,264},{264,8},{16,272},{272,16},{24,280},{280,24... | collective-permute-start | bytes 12296 | tf_op jit(solution)/shard_map/ppermute | solution.py:37
  39.2 0.7 copy-start.18
  42.3 63.7 %all-to-all-start = ((f32[64,8,512]{2,1,0:T(8,128)}), f32[64,8,512]{2,1,0:T(8,128)S(1)}, u32[]{:S(2)}, u32[]{:S(2)}) async-start(f32[64,8,512]{2,1,0:T(8,128)} %stack.103), calls=%async_computation | async-start | bytes 2097152 | tf_op jit(solution)/shard_map/all_to_all | solution.py:192
  52.0 0.7 copy-start.15
  54.5 1.1 copy-start.14
  72.8 1.3 %copy-start.9 = (f32[1,8,16,1]{2,1,3,0:T(8,128)S(1)}, f32[1,8,16,1]{2,1,3,0:T(8,128)}, u32[]{:S(2)}) copy-start(f32[1,8,16,1]{2,1,3,0:T(8,128)} %stack.76) | copy-start | bytes 1540
  74.1 0.7 copy-start.8
  74.8 0.7 copy-start.7
  75.4 0.7 copy-start.6
  76.1 0.7 copy-start.4
  76.8 0.7 copy-start.5
  77.5 0.7 copy-start.17
  91.4 0.6 copy-start.12
  92.1 0.8 copy-start.1
  106.0 0.7 copy-start.10
  106.3 0.7 copy-start.13
  110.6 0.8 copy-start.2
  110.7 0.7 copy-start.16
  (1 other events, 0.6 us)
